TPU v7x, 256 devices: a whole 4x4x8 slice. The times are simulated.
256 devices in a mesh: feed: 128 (over z_lo, x, y, core), tm: 2 (over z_hi).
Axes of the slice: x: 4, y: 4, z: 8 (z_hi: 2, z_lo: 4; z = z_hi * 4 + z_lo), core: 2. Of those that a mesh axis runs over, the one named last changes fastest.
Arguments:
- samples: bfloat16 [2048, 12288], P('feed', 'tm'), may hold values from -6 to 6
- filter_taps: float32 [4, 1024], replicated, may hold values from -3 to 3
- feed_cylinder: int32 [2048], replicated, may hold values from 0 to 3
- feed_delay: int32 [2048], replicated, may hold values from 0 to 4095
- pointing: int32 [512, 4], replicated, may hold values from 0 to 4095
- chirp_rate: float32 [512], P('feed'), may hold values from 1 to 40
Outputs:
- series: float32 [512, 12, 1024], P('feed', 'tm')
All inputs are finite; a program needn't handle non-finite values.
Results may differ from a plain program's by a relative error of at most 0.0046.
Values may be sent and summed in bfloat16 or wider, within the bound.
A program may use at most 64 MiB of HBM per device.

v0:
```python
import math

import jax
import jax.numpy as jnp
import numpy as np
from jax import lax
from jax.experimental import pallas as pl
from jax.experimental.pallas import tpu as pltpu
from jax.sharding import PartitionSpec as P

FEEDS = 2048
NCHAN = 512
BEAMS = 512
TAPS = 4
CYL = 4
PHASES = 4096
GROUPS = 128
NDEV = 256
MESH = pl.DeviceIdType.MESH
BF = jnp.bfloat16
F32 = jnp.float32
VMEM = pl.BlockSpec(memory_space=pltpu.VMEM)

def _fit():
    grid = np.cos(np.pi * (np.arange(4000) + 0.5) / 8000) * 0.5
    sq = grid * grid
    sine = np.sin(np.pi * grid) / grid * math.sqrt(2.0)
    cosine = np.cos(np.pi * grid) * math.sqrt(2.0)
    mat = np.stack([sq**k for k in range(5)], axis=1)
    s = np.linalg.lstsq(mat * grid[:, None], sine * grid, rcond=None)[0]
    c = np.linalg.lstsq(mat, cosine, rcond=None)[0]
    return [float(v) for v in s], [float(v) for v in c]


SIN_C, COS_C = _fit()
ROUND = 1.5 * 2.0**23


def cos_sin(turns):
    r = turns - ((turns + ROUND) - ROUND)
    q = r * r
    s = SIN_C[4]
    c = COS_C[4]
    for k in (3, 2, 1, 0):
        s = s * q + SIN_C[k]
        c = c * q + COS_C[k]
    s = s * r
    return 1.0 - s * s, s * c


def split_const(x):
    hi = x.astype(np.float32).astype(BF)
    lo = (x - hi.astype(np.float64)).astype(np.float32).astype(BF)
    return np.stack([hi, lo])


def forward_rows():
    n = np.arange(NCHAN)[None, :]
    out = []
    for par in range(2):
        c = 2 * np.arange(NCHAN // 2)[:, None] + par
        ang = (n * c % (2 * NCHAN)) * (2.0 * np.pi / (2 * NCHAN))
        both = np.stack([np.cos(ang), -np.sin(ang)], axis=1) / math.sqrt(2 * NCHAN)
        out.append(both.reshape(NCHAN, NCHAN))
    return split_const(np.stack(out))


def inverse_rows():
    t = np.arange(NCHAN // 2)[None, :]
    out = []
    for par in range(2):
        c = 2 * np.arange(NCHAN // 2)[:, None] + par
        ang = (t * c % NCHAN) * (2.0 * np.pi / NCHAN)
        out.append(np.concatenate([np.cos(ang), np.sin(ang)], axis=1) / math.sqrt(NCHAN))
    return split_const(np.stack(out))


def split(x):
    hi = x.astype(BF)
    return hi, (x - hi.astype(F32)).astype(BF)


def nt(a, b):
    return lax.dot_general(a, b, (((1,), (1,)), ((), ())), preferred_element_type=F32)


def dft_kernel(x_ref, tail_ref, taps_ref, basis_ref, o_ref, fold):
    length = 2 * NCHAN
    fold[...] = jnp.zeros_like(fold)
    for f in range(6):
        acc = None
        for k in range(TAPS):
            src = f + k - 3
            if src < 0:
                piece = tail_ref[:, (src + 3) * length : (src + 4) * length]
            else:
                piece = x_ref[:, src * length : (src + 1) * length]
            term = taps_ref[k : k + 1, :] * piece.astype(F32)
            acc = term if acc is None else acc + term
        a, b = acc[:, :NCHAN], acc[:, NCHAN:]
        fold[0, f * 16 : f * 16 + 16, :] = a + b
        fold[1, f * 16 : f * 16 + 16, :] = a - b
    for par in range(2):
        hi, lo = split(fold[par])
        top = basis_ref[0, par]
        out = nt(top, hi) + nt(top, lo) + nt(basis_ref[1, par], hi)
        o_ref[par] = out.astype(BF).reshape(NDEV, 2, 128)


def exchange_kernel(strided, x_ref, o_ref, send_sem, recv_sem):
    feed = lax.axis_index("feed")
    tm = lax.axis_index("tm")
    me = tm * GROUPS + feed
    barrier = pltpu.get_barrier_semaphore()

    def place(k):
        return lax.rem(feed + k, GROUPS), lax.rem(tm + (feed + k) // GROUPS, 2)

    def signal(k, carry):
        f, t = place(k)
        pl.semaphore_signal(barrier, inc=1, device_id=(f, t), device_id_type=MESH)
        return carry

    def view(ref, at):
        return ref.at[:, at] if strided else ref.at[at]

    def send(k, carry):
        f, t = place(k)
        pltpu.make_async_remote_copy(
            src_ref=view(x_ref, t * GROUPS + f), dst_ref=view(o_ref, me),
            send_sem=send_sem, recv_sem=recv_sem, device_id=(f, t), device_id_type=MESH,
        ).start()
        return carry

    lax.fori_loop(1, NDEV, signal, 0, unroll=15)
    pl.semaphore_wait(barrier, NDEV - 1)
    lax.fori_loop(1, NDEV, send, 0, unroll=15)
    if strided:
        o_ref[:, me] = x_ref[:, me]
    else:
        o_ref[me] = x_ref[me]
    some = (lambda r: r.at[:, pl.ds(0, NDEV - 1)]) if strided else (lambda r: r.at[pl.ds(0, NDEV - 1)])
    pltpu.make_async_remote_copy(
        src_ref=some(x_ref), dst_ref=some(o_ref), send_sem=send_sem, recv_sem=recv_sem,
        device_id=(feed, tm), device_id_type=MESH,
    ).wait()


def exchange(x, cid):
    import functools
    return pl.pallas_call(
        functools.partial(exchange_kernel, x.ndim == 4),
        out_shape=jax.ShapeDtypeStruct(x.shape, x.dtype),
        in_specs=[VMEM], out_specs=VMEM,
        scratch_shapes=[pltpu.SemaphoreType.DMA, pltpu.SemaphoreType.DMA],
        compiler_params=pltpu.CompilerParams(collective_id=cid, has_side_effects=True),
    )(x)


def beam_kernel(r_ref, delay_ref, cyl_ref, point_ref, o_ref, w_ref, wide, turned, lhs):
    m = lax.axis_index("tm") * GROUPS + lax.axis_index("feed")
    delay = delay_ref[...].astype(F32)
    cyl = cyl_ref[...]
    turns = []
    for par in range(2):
        t = (2 * m + par + 1).astype(F32) * delay
        turns.append(t - jnp.floor(t * (1.0 / PHASES)) * PHASES)
    point = point_ref[...].astype(F32) * (1.0 / PHASES)
    for i in range(16):
        kind = jnp.broadcast_to(cyl[:, i : i + 1], (GROUPS, 128))
        t0 = jnp.broadcast_to(turns[0][:, i : i + 1], (GROUPS, 128))
        t1 = jnp.broadcast_to(turns[1][:, i : i + 1], (GROUPS, 128))
        for lt in range(4):
            lanes = slice(lt * 128, lt * 128 + 128)
            p = point[:, lanes]
            steer = jnp.where(kind == 0, p[0:1], jnp.where(kind == 1, p[1:2], jnp.where(kind == 2, p[2:3], p[3:4])))
            for par, t in ((0, t0), (1, t1)):
                c, s = cos_sin(t * steer)
                w_ref[par, i * 128 : i * 128 + 128, lt * 128 : lt * 128 + 128] = c.astype(BF)
                w_ref[par, i * 128 : i * 128 + 128, 512 + lt * 128 : 512 + lt * 128 + 128] = s.astype(BF)
    for par in range(2):
        wide[...] = r_ref[par].astype(F32).reshape(2 * NDEV, 128)
        for ri in range(2):
            for tm in range(2):
                block = wide[pl.ds(tm * 256 + ri, 128, stride=2), :]
                turned[(ri * 2 + tm) * 128 : (ri * 2 + tm) * 128 + 128, :] = block.T
        for i in range(16):
            lhs[:, i * 128 : i * 128 + 128] = turned[pl.ds(i, 32, stride=16), :].astype(BF)
        prod = jnp.dot(lhs[...], w_ref[par], preferred_element_type=F32)
        scale = 1.0 / math.sqrt(FEEDS)
        real = (prod[:16, :512] - prod[16:, 512:]) * scale
        imag = (prod[:16, 512:] + prod[16:, :512]) * scale
        for tm in range(2):
            o_ref[tm * 32 + par * 16 : tm * 32 + par * 16 + 8, :] = real[tm * 8 : tm * 8 + 8]
            o_ref[tm * 32 + par * 16 + 8 : tm * 32 + par * 16 + 16, :] = imag[tm * 8 : tm * 8 + 8]


def pack_kernel(b_ref, o_ref, flip, wide):
    flip[...] = jnp.zeros_like(flip)
    for q in range(4):
        block = jnp.concatenate([b_ref[:, q * 128 : q * 128 + 128], jnp.zeros((64, 128), F32)], axis=0)
        flip[q * 128 : q * 128 + 128, :] = block.T
    wide[...] = jnp.zeros_like(wide)
    for tm in range(2):
        acc = None
        lane = lax.broadcasted_iota(jnp.int32, (128, 128), 1) // 32
        for b in range(4):
            rows = flip[pl.ds(b, 128, stride=4), :]
            moved = pltpu.roll(rows, (32 * (b - tm)) % 128, 1)
            acc = moved if acc is None else jnp.where(lane == b, moved, acc)
        wide[pl.ds(tm * 256, 128, stride=2), :] = acc
    o_ref[...] = wide[...].astype(BF).reshape(NDEV, 2, 128)


def synth_kernel(q_ref, rate_ref, basis_ref, o_ref, wide, turned):
    wide[...] = q_ref[...].astype(F32).reshape(2 * NDEV, 128)
    for h in range(2):
        turned[:, h * 128 : h * 128 + 128] = wide[pl.ds(h * 256, 128, stride=2), :].T
    s = lax.broadcasted_iota(jnp.int32, (8, 256), 1)
    halves = []
    for par in range(2):
        pos = (2 * s + par).astype(F32) * (1.0 / NCHAN)
        real, imag = [], []
        for b in range(4):
            c, sn = cos_sin((0.5 * rate_ref[b]) * (pos * pos))
            at = b * 32 + par * 16
            xr = turned[at : at + 8, :]
            xi = turned[at + 8 : at + 16, :]
            real.append(xr * c - xi * sn)
            imag.append(xr * sn + xi * c)
        both = jnp.concatenate(real + imag, axis=0)
        hi, lo = split(both)
        top = basis_ref[0, par]
        prod = (
            jnp.dot(hi, top, preferred_element_type=F32)
            + jnp.dot(lo, top, preferred_element_type=F32)
            + jnp.dot(hi, basis_ref[1, par], preferred_element_type=F32)
        )
        halves.append((prod[:32, :256] - prod[32:, 256:], prod[:32, 256:] + prod[32:, :256]))
    (er, ei), (orr, oi) = halves
    for b in range(4):
        rows = slice(b * 8, b * 8 + 6)
        o_ref[b, :, 0:256] = er[rows] + orr[rows]
        o_ref[b, :, 256:512] = er[rows] - orr[rows]
        o_ref[b, :, 512:768] = ei[rows] + oi[rows]
        o_ref[b, :, 768:1024] = ei[rows] - oi[rows]


def body(samples, filter_taps, feed_cylinder, feed_delay, pointing, chirp_rate):
    tail = lax.ppermute(samples[:, 3 * 2 * NCHAN :], "tm", [(0, 1)])
    big = pltpu.CompilerParams(vmem_limit_bytes=56 * 2**20)
    sent = pl.pallas_call(
        dft_kernel,
        out_shape=jax.ShapeDtypeStruct((2, NDEV, 2, 128), BF),
        in_specs=[VMEM] * 4, out_specs=VMEM,
        scratch_shapes=[pltpu.VMEM((2, 128, NCHAN), F32)],
        compiler_params=big,
    )(samples, tail, filter_taps, jnp.asarray(forward_rows()))
    got = exchange(sent, 0)
    formed = pl.pallas_call(
        beam_kernel,
        out_shape=jax.ShapeDtypeStruct((64, BEAMS), F32),
        in_specs=[VMEM] * 4, out_specs=VMEM,
        scratch_shapes=[
            pltpu.VMEM((2, FEEDS, 2 * BEAMS), BF),
            pltpu.VMEM((2 * NDEV, 128), F32),
            pltpu.VMEM((512, 128), F32),
            pltpu.VMEM((32, FEEDS), BF),
        ],
        compiler_params=big,
    )(got, feed_delay.reshape(GROUPS, 16), feed_cylinder.reshape(GROUPS, 16), pointing.T)
    packed = pl.pallas_call(
        pack_kernel,
        out_shape=jax.ShapeDtypeStruct((NDEV, 2, 128), BF),
        in_specs=[VMEM], out_specs=VMEM,
        scratch_shapes=[pltpu.VMEM((512, 128), F32), pltpu.VMEM((512, 128), F32)],
        compiler_params=big,
    )(formed)
    back = exchange(packed, 1)
    return pl.pallas_call(
        synth_kernel,
        out_shape=jax.ShapeDtypeStruct((4, 6, 2 * NCHAN), F32),
        in_specs=[VMEM, pl.BlockSpec(memory_space=pltpu.SMEM), VMEM], out_specs=VMEM,
        scratch_shapes=[pltpu.VMEM((2 * NDEV, 128), F32), pltpu.VMEM((128, 256), F32)],
        compiler_params=big,
    )(back, chirp_rate, jnp.asarray(inverse_rows()))


def solution(mesh):
    return jax.shard_map(
        body,
        mesh=mesh,
        in_specs=(P("feed", "tm"), P(), P(), P(), P(), P("feed")),
        out_specs=P("feed", "tm", None),
        check_vma=False,
    )
```

profile of v0, /device:TPU:1, one launch (start us, length us, event | category | flops | bytes accessed | tf_op | source)
XLA Modules:
  0.0 79.1 jit_solution(12225358860066954977)
XLA Ops:
  0.0 0.9 %slice.3 = bf16[16,3072]{1,0:T(8,128)(2,1)S(1)} slice(bf16[16,6144]{1,0:T(8,128)(2,1)} %x_ref.1), slice={[0:16], [3072:6144]} | slice | bytes 196608 | tf_op jit(solution)/shard_map/slice | solution.py:250
  0.9 9.6 %collective-permute-start = (bf16[16,3072]{1,0:T(8,128)(2,1)S(1)}, bf16[16,3072]{1,0:T(8,128)(2,1)S(1)}, u32[]{:S(2)}, u32[]{:S(2)}) collective-permute-start(bf16[16,3072]{1,0:T(8,128)(2,1)S(1)} %slice.3), channel_id=1, source_target_pairs={{0,1},{2,3},{4,5},{6,7},{8,9},{10,11},{12,13},{14,15},{16,17},{18,... | collective-permute-start | bytes 294920 | tf_op jit(solution)/shard_map/ppermute | solution.py:250
  10.5 1.4 %reshape.6.delay_ref = s32[128,16]{1,0:T(8,128)} reshape(s32[2048]{0:T(1024)} %param.11) | data formatting | bytes 16384 | tf_op jit(solution)/shard_map/reshape | solution.py:271
  11.9 1.4 %reshape.7.cyl_ref = s32[128,16]{1,0:T(8,128)} reshape(s32[2048]{0:T(1024)} %param.10) | data formatting | bytes 16384 | tf_op jit(solution)/shard_map/reshape | solution.py:271
  13.3 0.0 collective-permute-done.tail_ref
  13.3 0.0 copy-start
  13.3 0.6 copy-done
  14.0 3.6 %shard_map.82.x_ref = bf16[2,256,2,128]{3,2,1,0:T(2,128)(2,1)} custom-call(bf16[16,6144]{1,0:T(8,128)(2,1)} %x_ref.1, bf16[16,3072]{1,0:T(8,128)(2,1)} %copy-done, f32[4,1024]{1,0:T(4,128)} %taps_ref.1, bf16[2,2,512,512]{3,2,1,0:T(8,128)(2,1)} %constant.4.clone.basis_ref), custom_call_target="tpu_custom_call" | custom-call | tf_op jit(solution)/shard_map/pallas_call | solution.py:252
  17.5 26.4 %shard_map.83.r_ref = bf16[2,256,2,128]{3,2,1,0:T(2,128)(2,1)} custom-call(bf16[2,256,2,128]{3,2,1,0:T(2,128)(2,1)} %shard_map.82.x_ref), custom_call_target="tpu_custom_call" | custom-call | tf_op jit(solution)/shard_map/pallas_call | solution.py:151
  43.9 11.0 %shard_map.84.b_ref = f32[64,512]{1,0:T(8,128)} custom-call(bf16[2,256,2,128]{3,2,1,0:T(2,128)(2,1)} %shard_map.83.r_ref, s32[128,16]{1,0:T(8,128)} %reshape.6.delay_ref, s32[128,16]{1,0:T(8,128)} %reshape.7.cyl_ref, s32[4,512]{1,0:T(4,128)} %bitcast.1), custom_call_target="tpu_custom_call" | custom-call | tf_op jit(solution)/shard_map/pallas_call | solution.py:260
  54.9 1.9 %shard_map.85.x_ref = bf16[256,2,128]{2,1,0:T(2,128)(2,1)} custom-call(f32[64,512]{1,0:T(8,128)} %shard_map.84.b_ref), custom_call_target="tpu_custom_call" | custom-call | tf_op jit(solution)/shard_map/pallas_call | solution.py:272
  56.8 18.2 %shard_map.86.q_ref = bf16[256,2,128]{2,1,0:T(2,128)(2,1)} custom-call(bf16[256,2,128]{2,1,0:T(2,128)(2,1)} %shard_map.85.x_ref), custom_call_target="tpu_custom_call" | custom-call | tf_op jit(solution)/shard_map/pallas_call | solution.py:151
  75.0 2.5 %shard_map.87 = f32[4,6,1024]{2,1,0:T(8,128)} custom-call(bf16[256,2,128]{2,1,0:T(2,128)(2,1)} %shard_map.86.q_ref, f32[4]{0:T(128)} %rate_ref.1, bf16[2,2,256,512]{3,2,1,0:T(8,128)(2,1)} %constant.5.clone.basis_ref), custom_call_target="tpu_custom_call" | custom-call | tf_op jit(solution)/shard_map/pallas_call | solution.py:280
  77.5 1.6 %copy.10 = f32[4,6,1024]{2,0,1:T(4,128)} copy(f32[4,6,1024]{2,1,0:T(8,128)} %shard_map.87) | data formatting | bytes 196608 | tf_op jit(solution)/shard_map/pallas_call | solution.py:280
Async XLA Ops:
  0.9 12.4 %collective-permute-start = (bf16[16,3072]{1,0:T(8,128)(2,1)S(1)}, bf16[16,3072]{1,0:T(8,128)(2,1)S(1)}, u32[]{:S(2)}, u32[]{:S(2)}) collective-permute-start(bf16[16,3072]{1,0:T(8,128)(2,1)S(1)} %slice.3), channel_id=1, source_target_pairs={{0,1},{2,3},{4,5},{6,7},{8,9},{10,11},{12,13},{14,15},{16,17},{18,... | collective-permute-start | bytes 294920 | tf_op jit(solution)/shard_map/ppermute | solution.py:250
  13.3 0.6 copy-start
where the time goes:
time: 79.4 us; the launch traced here: 79.1 us
  Pallas kernels  63.5 us (80%)
  starting transfers between devices  9.62 us (12%)
  local copies, waits for them, and re-layouts  5.94 us (7%)
    pallas_call x2, Pallas kernels, exchange(): pl.pallas_call(functools.partial(exchange_kernel, x.ndim == 4), out_shape...  44.6 us
    pallas_call x1, Pallas kernels, body(): pl.pallas_call(beam_kernel, out_shape=jax.ShapeDtypeStruct((64, BEAMS), F...  11 us
    ppermute x1, starting transfers between devices, body(): tail = lax.ppermute(samples[:, 3 * 2 * NCHAN:], 'tm', [(0, 1)])  9.62 us
    pallas_call x1, Pallas kernels, body(): pl.pallas_call(dft_kernel, out_shape=jax.ShapeDtypeStruct((2, NDEV, 2, 12...  3.55 us
    pallas_call x1, Pallas kernels, body(): pl.pallas_call(synth_kernel, out_shape=jax.ShapeDtypeStruct((4, 6, 2 * NC...  2.46 us
    pallas_call x1, Pallas kernels, body(): pl.pallas_call(pack_kernel, out_shape=jax.ShapeDtypeStruct((NDEV, 2, 128)...  1.89 us
    pallas_call x1, local copies, waits for them, and re-layouts, body(): pl.pallas_call(synth_kernel, out_shape=jax.ShapeDtypeStruct((4, 6, 2 * NC...  1.61 us
  transfers between devices with their start and end apart: 1, of which 0 were waited for; matrix products, arithmetic and copies ran while one was open for 4% of the time, Pallas kernels for 0%

commit v1 on v0

v1 whole, which is shorter than its diff:
```python
import math

import jax
import jax.numpy as jnp
import numpy as np
from jax import lax
from jax.experimental import pallas as pl
from jax.experimental.pallas import tpu as pltpu
from jax.sharding import PartitionSpec as P

FEEDS = 2048
NCHAN = 512
BEAMS = 512
TAPS = 4
CYL = 4
PHASES = 4096
GROUPS = 128
NDEV = 256
MESH = pl.DeviceIdType.MESH
BF = jnp.bfloat16
F32 = jnp.float32
VMEM = pl.BlockSpec(memory_space=pltpu.VMEM)

def _fit():
    grid = np.cos(np.pi * (np.arange(4000) + 0.5) / 8000) * 0.5
    sq = grid * grid
    sine = np.sin(np.pi * grid) / grid * math.sqrt(2.0)
    cosine = np.cos(np.pi * grid) * math.sqrt(2.0)
    mat = np.stack([sq**k for k in range(5)], axis=1)
    s = np.linalg.lstsq(mat * grid[:, None], sine * grid, rcond=None)[0]
    c = np.linalg.lstsq(mat, cosine, rcond=None)[0]
    return [float(v) for v in s], [float(v) for v in c]


SIN_C, COS_C = _fit()
ROUND = 1.5 * 2.0**23
EARLY = 17
PER = 17


def cos_sin(turns):
    r = turns - ((turns + ROUND) - ROUND)
    q = r * r
    s = SIN_C[4]
    c = COS_C[4]
    for k in (3, 2, 1, 0):
        s = s * q + SIN_C[k]
        c = c * q + COS_C[k]
    s = s * r
    return 1.0 - s * s, s * c


def split_const(x):
    hi = x.astype(np.float32).astype(BF)
    lo = (x - hi.astype(np.float64)).astype(np.float32).astype(BF)
    return np.stack([hi, lo])


def forward_rows():
    n = np.arange(NCHAN)[None, :]
    out = []
    for par in range(2):
        c = 2 * np.arange(NCHAN // 2)[:, None] + par
        ang = (n * c % (2 * NCHAN)) * (2.0 * np.pi / (2 * NCHAN))
        both = np.stack([np.cos(ang), -np.sin(ang)], axis=1) / math.sqrt(2 * NCHAN)
        out.append(both.reshape(NCHAN, NCHAN))
    return split_const(np.stack(out))


def inverse_rows():
    t = np.arange(NCHAN // 2)[None, :]
    out = []
    for par in range(2):
        c = 2 * np.arange(NCHAN // 2)[:, None] + par
        ang = (t * c % NCHAN) * (2.0 * np.pi / NCHAN)
        out.append(np.concatenate([np.cos(ang), np.sin(ang)], axis=1) / math.sqrt(NCHAN))
    return split_const(np.stack(out))


def split(x):
    hi = x.astype(BF)
    return hi, (x - hi.astype(F32)).astype(BF)


def nt(a, b):
    return lax.dot_general(a, b, (((1,), (1,)), ((), ())), preferred_element_type=F32)


def main_kernel(
    x_ref, taps_ref, delay_ref, cyl_ref, point_ref, basis_ref, back_ref,
    tail, basis, fold, sent, got, weights, cols, table, wide, turned, lhs, flip, pairs, packed,
    load_sem, halo_send, halo_recv, ready, send_sem, recv_sem,
):
    length = 2 * NCHAN
    feed = lax.axis_index("feed")
    tm = lax.axis_index("tm")
    me = tm * GROUPS + feed
    plane = lax.rem(feed // 2, 16)
    ring = tm * 8 + feed // 32 * 2 + lax.rem(feed, 2)

    def at(ring, plane):
        return lax.rem(ring // 2, 4) * 32 + plane * 2 + lax.rem(ring, 2), ring // 8

    load = pltpu.make_async_copy(basis_ref, basis, load_sem)
    load.start()
    barrier = pltpu.get_barrier_semaphore()
    for k in range(1, 16):
        for where in (at(ring ^ k, plane), at(ring, plane ^ k)):
            pl.semaphore_signal(barrier, inc=1, device_id=where, device_id_type=MESH)

    delay = delay_ref[...].astype(F32)
    cyl = cyl_ref[...].astype(F32)
    for par in range(2):
        t = (2 * me + par + 1).astype(F32) * delay
        t = t - jnp.floor(t * (1.0 / PHASES)) * PHASES
        for g in range(8):
            cols[par, pl.ds(g, 16, stride=8), :] = pltpu.roll(t, (128 - 16 * g) % 128, 1)
    for g in range(8):
        cols[2, pl.ds(g, 16, stride=8), :] = pltpu.roll(cyl, (128 - 16 * g) % 128, 1)
    for q in range(4):
        table[q, 0:4, :] = point_ref[:, q * 128 : q * 128 + 128].astype(F32) * (1.0 / PHASES)
    fold[...] = jnp.zeros_like(fold)

    pl.semaphore_wait(barrier, 30)
    for k in range(1, 16):
        pl.semaphore_signal(ready, inc=1, device_id=at(ring, plane ^ k), device_id_type=MESH)
    halo = pltpu.make_async_remote_copy(
        src_ref=x_ref.at[:, pl.ds(3 * length, 3 * length)], dst_ref=tail,
        send_sem=halo_send, recv_sem=halo_recv, device_id=(feed, 1), device_id_type=MESH,
    )

    @pl.when(tm == 0)
    def _():
        halo.start()
        tail[...] = jnp.zeros_like(tail)

    def make(step):
        i, half = step // 2, lax.rem(step, 2)
        shift = lax.rem(128 - i, 128)
        for rc in range(4):
            rows = slice(rc * 32, rc * 32 + 32)
            t0, t1, kind = [
                jnp.broadcast_to(pltpu.roll(cols[n, rows, :], shift, 1)[:, 0:1], (32, 128)) for n in range(3)
            ]
            for j in range(2):
                q = half * 2 + j
                p = [table[q, k : k + 1, :] for k in range(4)]
                steer = jnp.where(kind == 0.0, p[0], jnp.where(kind == 1.0, p[1], jnp.where(kind == 2.0, p[2], p[3])))
                for par, t in ((0, t0), (1, t1)):
                    c, s = cos_sin(t * steer)
                    at_rows = pl.ds(pl.multiple_of(i * 128 + rc * 32, 32), 32)
                    weights[par, q, at_rows, 0:128] = c.astype(BF)
                    weights[par, q, at_rows, 128:256] = s.astype(BF)

    def early(step, carry):
        make(step)
        return carry

    lax.fori_loop(0, EARLY, early, 0)
    load.wait()

    @pl.when(tm == 1)
    def _():
        halo.wait_recv()

    for f in range(6):
        acc = None
        for k in range(TAPS):
            src = f + k - 3
            if src < 0:
                piece = tail[:, (src + 3) * length : (src + 4) * length]
            else:
                piece = x_ref[:, src * length : (src + 1) * length]
            term = taps_ref[k : k + 1, :] * piece.astype(F32)
            acc = term if acc is None else acc + term
        a, b = acc[:, :NCHAN], acc[:, NCHAN:]
        fold[0, f * 16 : f * 16 + 16, :] = a + b
        fold[1, f * 16 : f * 16 + 16, :] = a - b
    for par in range(2):
        hi, lo = split(fold[par])
        top = basis[0, par]
        out = nt(top, hi) + nt(top, lo) + nt(basis[1, par], hi)
        sent[par] = out.astype(BF).reshape(NDEV, 2, 128)

    @pl.when(tm == 0)
    def _():
        halo.wait_send()

    pl.semaphore_wait(ready, 15)

    def late(step, carry):
        for n in range(PER):
            k = 1 + step * PER + n
            f, t = lax.rem(feed + k, GROUPS), lax.rem(tm + (feed + k) // GROUPS, 2)
            pltpu.make_async_remote_copy(
                src_ref=sent.at[:, t * GROUPS + f], dst_ref=got.at[:, me],
                send_sem=send_sem.at[0], recv_sem=recv_sem.at[0], device_id=(f, t), device_id_type=MESH,
            ).start()
        make(EARLY + step)
        return carry

    lax.fori_loop(0, 32 - EARLY, late, 0)
    got[:, me] = sent[:, me]
    pltpu.make_async_remote_copy(
        src_ref=sent.at[:, pl.ds(0, NDEV - 1)], dst_ref=got.at[:, pl.ds(0, NDEV - 1)],
        send_sem=send_sem.at[0], recv_sem=recv_sem.at[0], device_id=(feed, tm), device_id_type=MESH,
    ).wait()

    for par in range(2):
        wide[...] = got[par].astype(F32).reshape(2 * NDEV, 128)
        for ri in range(2):
            for t in range(2):
                block = wide[pl.ds(t * 256 + ri, 128, stride=2), :]
                turned[(ri * 2 + t) * 128 : (ri * 2 + t) * 128 + 128, :] = block.T
        for i in range(16):
            lhs[par, :, i * 128 : i * 128 + 128] = turned[pl.ds(i, 32, stride=16), :].astype(BF)

    pairs[...] = jnp.zeros_like(pairs)
    scale = 1.0 / math.sqrt(FEEDS)
    lane = lax.broadcasted_iota(jnp.int32, (32, 128), 1) // 32

    def chunk(step, carry):
        q = lax.rem(step + feed // 32, 4)
        parts = []
        for par in range(2):
            prod = jnp.dot(lhs[par], weights[par, q], preferred_element_type=F32)
            real = (prod[:16, :128] - prod[16:, 128:]) * scale
            imag = (prod[:16, 128:] + prod[16:, :128]) * scale
            parts.append((real, imag))
        rows = [parts[par][ri][t * 8 : t * 8 + 8] for t in range(2) for par in range(2) for ri in range(2)]
        flip[...] = jnp.concatenate(rows + [jnp.zeros((64, 128), F32)], axis=0).T
        for t in range(2):
            acc = None
            for b in range(4):
                moved = flip[pl.ds(b, 32, stride=4), :]
                if b != t:
                    moved = pltpu.roll(moved, (32 * (b - t)) % 128, 1)
                acc = moved if acc is None else jnp.where(lane == b, moved, acc)
            pairs[pl.ds(0, 32, stride=2), :] = acc
            packed[pl.ds(t * GROUPS + q * 32, 32)] = pairs[...].astype(BF).reshape(32, 2, 128)

        def send(n, carry):
            v = lax.rem(n + feed, 64)
            t, f = v // 32, q * 32 + lax.rem(v, 32)
            to = t * GROUPS + f

            @pl.when(to != me)
            def _():
                pltpu.make_async_remote_copy(
                    src_ref=packed.at[to], dst_ref=back_ref.at[me],
                    send_sem=send_sem.at[1], recv_sem=recv_sem.at[1], device_id=(f, t), device_id_type=MESH,
                ).start()

            return carry

        lax.fori_loop(0, 64, send, 0, unroll=16)
        return carry

    lax.fori_loop(0, 4, chunk, 0)
    back_ref[me] = packed[me]
    pltpu.make_async_remote_copy(
        src_ref=packed.at[pl.ds(0, NDEV - 1)], dst_ref=back_ref.at[pl.ds(0, NDEV - 1)],
        send_sem=send_sem.at[1], recv_sem=recv_sem.at[1], device_id=(feed, tm), device_id_type=MESH,
    ).wait()


def synth_kernel(q_ref, rate_ref, basis_ref, o_ref, wide, turned):
    wide[...] = q_ref[...].astype(F32).reshape(2 * NDEV, 128)
    for h in range(2):
        turned[:, h * 128 : h * 128 + 128] = wide[pl.ds(h * 256, 128, stride=2), :].T
    s = lax.broadcasted_iota(jnp.int32, (8, 256), 1)
    halves = []
    for par in range(2):
        pos = (2 * s + par).astype(F32) * (1.0 / NCHAN)
        real, imag = [], []
        for b in range(4):
            c, sn = cos_sin((0.5 * rate_ref[b]) * (pos * pos))
            at = b * 32 + par * 16
            xr = turned[at : at + 8, :]
            xi = turned[at + 8 : at + 16, :]
            real.append(xr * c - xi * sn)
            imag.append(xr * sn + xi * c)
        both = jnp.concatenate(real + imag, axis=0)
        hi, lo = split(both)
        top = basis_ref[0, par]
        prod = (
            jnp.dot(hi, top, preferred_element_type=F32)
            + jnp.dot(lo, top, preferred_element_type=F32)
            + jnp.dot(hi, basis_ref[1, par], preferred_element_type=F32)
        )
        halves.append((prod[:32, :256] - prod[32:, 256:], prod[:32, 256:] + prod[32:, :256]))
    (er, ei), (orr, oi) = halves
    for b in range(4):
        rows = slice(b * 8, b * 8 + 6)
        o_ref[:, b, 0:256] = er[rows] + orr[rows]
        o_ref[:, b, 256:512] = er[rows] - orr[rows]
        o_ref[:, b, 512:768] = ei[rows] + oi[rows]
        o_ref[:, b, 768:1024] = ei[rows] - oi[rows]


def body(samples, filter_taps, feed_cylinder, feed_delay, pointing, chirp_rate):
    back = pl.pallas_call(
        main_kernel,
        out_shape=jax.ShapeDtypeStruct((NDEV, 2, 128), BF),
        in_specs=[VMEM] * 5 + [pl.BlockSpec(memory_space=pl.ANY)], out_specs=VMEM,
        scratch_shapes=[
            pltpu.VMEM((16, 3 * 2 * NCHAN), BF),
            pltpu.VMEM((2, 2, NCHAN, NCHAN), BF),
            pltpu.VMEM((2, 128, NCHAN), F32),
            pltpu.VMEM((2, NDEV, 2, 128), BF),
            pltpu.VMEM((2, NDEV, 2, 128), BF),
            pltpu.VMEM((2, 4, FEEDS, 256), BF),
            pltpu.VMEM((3, GROUPS, 128), F32),
            pltpu.VMEM((4, 8, 128), F32),
            pltpu.VMEM((2 * NDEV, 128), F32),
            pltpu.VMEM((512, 128), F32),
            pltpu.VMEM((2, 32, FEEDS), BF),
            pltpu.VMEM((128, 128), F32),
            pltpu.VMEM((64, 128), F32),
            pltpu.VMEM((NDEV, 2, 128), BF),
            pltpu.SemaphoreType.DMA,
            pltpu.SemaphoreType.DMA,
            pltpu.SemaphoreType.DMA,
            pltpu.SemaphoreType.REGULAR,
            pltpu.SemaphoreType.DMA((2,)),
            pltpu.SemaphoreType.DMA((2,)),
        ],
        compiler_params=pltpu.CompilerParams(collective_id=0, has_side_effects=True, vmem_limit_bytes=40 * 2**20),
    )(samples, filter_taps, feed_delay.reshape(16, 128), feed_cylinder.reshape(16, 128), pointing.T, jnp.asarray(forward_rows()))
    series = pl.pallas_call(
        synth_kernel,
        out_shape=jax.ShapeDtypeStruct((6, 4, 2 * NCHAN), F32),
        in_specs=[VMEM, pl.BlockSpec(memory_space=pltpu.SMEM), VMEM], out_specs=VMEM,
        scratch_shapes=[pltpu.VMEM((2 * NDEV, 128), F32), pltpu.VMEM((128, 256), F32)],
        compiler_params=pltpu.CompilerParams(vmem_limit_bytes=16 * 2**20),
    )(back, chirp_rate, jnp.asarray(inverse_rows()))
    return jnp.transpose(series, (1, 0, 2))


def solution(mesh):
    return jax.shard_map(
        body,
        mesh=mesh,
        in_specs=(P("feed", "tm"), P(), P(), P(), P(), P("feed")),
        out_specs=P("feed", "tm", None),
        check_vma=False,
    )
```

time: 79.4 us -> 53.3 us (0.67)
  Pallas kernels: 63.5 us -> 47.6 us
  starting transfers between devices: 9.62 us -> 0 us
    pallas_call x6 -> x2, Pallas kernels: 63.5 us -> 47.6 us  [the longest x1 45.8 us: body(): pl.pallas_call(main_kernel, out_shape=jax.ShapeDtypeStruct((NDEV, 2, 128)...]
    ppermute x1 -> x0, starting transfers between devices: 9.62 us -> none  [body(): tail = lax.ppermute(samples[:, 3 * 2 * NCHAN:], 'tm', [(0, 1)])]
    unnamed x2 -> x16, local copies, waits for them, and re-layouts: 0.64 us -> 5.34 us
    reshape x2 -> x0, local copies, waits for them, and re-layouts: 2.79 us -> none  [the longest x1 1.4 us: body(): feed_delay.reshape(GROUPS, 16)]
    pallas_call x1 -> x0, local copies, waits for them, and re-layouts: 1.61 us -> none  [body(): pl.pallas_call(synth_kernel, out_shape=jax.ShapeDtypeStruct((4, 6, 2 * NC...]
    slice x1 -> x0, local copies, waits for them, and re-layouts: 0.9 us -> none  [body(): tail = lax.ppermute(samples[:, 3 * 2 * NCHAN:], 'tm', [(0, 1)])]
  transfers between devices with their start and end apart: 1 -> 0, of which waited for: 0 -> 0; matrix products, arithmetic and copies ran while one was open for 4% -> 0% of each run, Pallas kernels for 0% -> 0%
where the time goes in v1:
time: 53.3 us; the launch traced here: 52.9 us
  Pallas kernels  47.6 us (89%)
  local copies, waits for them, and re-layouts  5.34 us (10%)
    pallas_call x1, Pallas kernels, body(): pl.pallas_call(main_kernel, out_shape=jax.ShapeDtypeStruct((NDEV, 2, 128)...  45.8 us
    unnamed x16, local copies, waits for them, and re-layouts  5.34 us
    pallas_call x1, Pallas kernels, body(): pl.pallas_call(synth_kernel, out_shape=jax.ShapeDtypeStruct((6, 4, 2 * NC...  1.72 us

profile of v1, /device:TPU:1, one launch (start us, length us, event | category | flops | bytes accessed | tf_op | source)
XLA Modules:
  0.0 52.9 jit_solution(14839578299258475563)
XLA Ops:
  0.0 0.0 copy-start.7
  0.0 0.0 copy-start
  0.0 1.6 %copy-done = bf16[2,2,512,512]{3,2,1,0:T(8,128)(2,1)S(1)} copy-done((bf16[2,2,512,512]{3,2,1,0:T(8,128)(2,1)S(1)}, bf16[2,2,512,512]{3,2,1,0:T(8,128)(2,1)}, u32[]{:S(2)}) %copy-start) | copy-done | bytes 2097176
  1.6 0.0 copy-start.2
  1.6 0.9 %copy-done.2 = bf16[16,6144]{1,0:T(8,128)(2,1)S(1)} copy-done((bf16[16,6144]{1,0:T(8,128)(2,1)S(1)}, bf16[16,6144]{1,0:T(8,128)(2,1)}, u32[]{:S(2)}) %copy-start.2) | copy-done | bytes 196632
  2.5 0.0 copy-start.3
  2.5 0.7 %copy-done.3 = f32[4,1024]{1,0:T(4,128)S(1)} copy-done((f32[4,1024]{1,0:T(4,128)S(1)}, f32[4,1024]{1,0:T(4,128)}, u32[]{:S(2)}) %copy-start.3) | copy-done | bytes 16408
  3.3 0.0 copy-start.4
  3.3 0.7 %copy-done.4 = s32[2048]{0:T(1024)S(1)} copy-done((s32[2048]{0:T(1024)S(1)}, s32[2048]{0:T(1024)}, u32[]{:S(2)}) %copy-start.4) | copy-done | bytes 8216
  4.0 0.0 copy-start.5
  4.0 0.7 %copy-done.5 = s32[2048]{0:T(1024)S(1)} copy-done((s32[2048]{0:T(1024)S(1)}, s32[2048]{0:T(1024)}, u32[]{:S(2)}) %copy-start.5) | copy-done | bytes 8216
  4.6 0.0 copy-start.6
  4.7 0.7 %copy-done.6 = s32[512,4]{0,1:T(4,128)S(1)} copy-done((s32[512,4]{0,1:T(4,128)S(1)}, s32[512,4]{0,1:T(4,128)}, u32[]{:S(2)}) %copy-start.6) | copy-done | bytes 8216
  5.3 0.0 copy-start.1
  5.3 45.8 %shard_map.82.q_ref = bf16[256,2,128]{2,1,0:T(2,128)(2,1)S(1)} custom-call(bf16[16,6144]{1,0:T(8,128)(2,1)S(1)} %copy-done.2, f32[4,1024]{1,0:T(4,128)S(1)} %copy-done.3, s32[16,128]{1,0:T(8,128)S(1)} %bitcast.4, s32[16,128]{1,0:T(8,128)S(1)} %bitcast.5, s32[4,512]{1,0:T(4,128)S(1)} %bitcast.6, bf16[2,2,512,512]{3,2,1,0:T(8,128)(2,1)S(1)} %copy-done), custom_call_target="tpu_custom_call" | custom-call | tf_op jit(solution)/shard_map/pallas_call | solution.py:302
  51.2 0.0 copy-done.7
  51.2 0.0 copy-done.1
  51.2 1.7 %shard_map.83 = f32[6,4,1024]{2,1,0:T(4,128)} custom-call(bf16[256,2,128]{2,1,0:T(2,128)(2,1)S(1)} %shard_map.82.q_ref, f32[4]{0:T(128)S(1)} %copy-done.7, bf16[2,2,256,512]{3,2,1,0:T(8,128)(2,1)S(1)} %copy-done.1), custom_call_target="tpu_custom_call" | custom-call | tf_op jit(solution)/shard_map/pallas_call | solution.py:330
Async XLA Ops:
  0.0 51.2 %copy-start.7 = (f32[4]{0:T(128)S(1)}, f32[4]{0:T(128)}, u32[]{:S(2)}) copy-start(f32[4]{0:T(128)} %rate_ref.1) | copy-start | bytes 52
  0.0 1.6 %copy-start = (bf16[2,2,512,512]{3,2,1,0:T(8,128)(2,1)S(1)}, bf16[2,2,512,512]{3,2,1,0:T(8,128)(2,1)}, u32[]{:S(2)}) copy-start(bf16[2,2,512,512]{3,2,1,0:T(8,128)(2,1)} %constant.4.clone.basis_ref) | copy-start | bytes 6291460
  1.6 0.9 %copy-start.2 = (bf16[16,6144]{1,0:T(8,128)(2,1)S(1)}, bf16[16,6144]{1,0:T(8,128)(2,1)}, u32[]{:S(2)}) copy-start(bf16[16,6144]{1,0:T(8,128)(2,1)} %x_ref.1) | copy-start | bytes 589828
  2.5 0.7 %copy-start.3 = (f32[4,1024]{1,0:T(4,128)S(1)}, f32[4,1024]{1,0:T(4,128)}, u32[]{:S(2)}) copy-start(f32[4,1024]{1,0:T(4,128)} %taps_ref.1) | copy-start | bytes 49156
  3.3 0.7 %copy-start.4 = (s32[2048]{0:T(1024)S(1)}, s32[2048]{0:T(1024)}, u32[]{:S(2)}) copy-start(s32[2048]{0:T(1024)} %param.11) | copy-start | bytes 24580
  4.0 0.7 %copy-start.5 = (s32[2048]{0:T(1024)S(1)}, s32[2048]{0:T(1024)}, u32[]{:S(2)}) copy-start(s32[2048]{0:T(1024)} %param.10) | copy-start | bytes 24580
  4.6 0.7 %copy-start.6 = (s32[512,4]{0,1:T(4,128)S(1)}, s32[512,4]{0,1:T(4,128)}, u32[]{:S(2)}) copy-start(s32[512,4]{0,1:T(4,128)} %param.12) | copy-start | bytes 24580
  5.3 45.9 %copy-start.1 = (bf16[2,2,256,512]{3,2,1,0:T(8,128)(2,1)S(1)}, bf16[2,2,256,512]{3,2,1,0:T(8,128)(2,1)}, u32[]{:S(2)}) copy-start(bf16[2,2,256,512]{3,2,1,0:T(8,128)(2,1)} %constant.5.clone.basis_ref) | copy-start | bytes 3145732

commit v2 on v1

--- a/solution.py
+++ b/solution.py
@@ -34,8 +34,9 @@
 
 SIN_C, COS_C = _fit()
 ROUND = 1.5 * 2.0**23
-EARLY = 17
+MAIN_VMEM = 62 * 2**20
 PER = 17
+MULT = 37
 
 
 def cos_sin(turns):
@@ -87,9 +88,9 @@
 
 
 def main_kernel(
-    x_ref, taps_ref, delay_ref, cyl_ref, point_ref, basis_ref, back_ref,
-    tail, basis, fold, sent, got, weights, cols, table, wide, turned, lhs, flip, pairs, packed,
-    load_sem, halo_send, halo_recv, ready, send_sem, recv_sem,
+    x_hbm, taps_hbm, delay_hbm, cyl_hbm, point_hbm, basis_hbm, back_ref,
+    x_ref, taps_ref, delay_ref, cyl_ref, point_ref, basis, fold, sent, got, weights, cols, table, wide, turned, lhs, flip, pairs, packed,
+    load_sem, ready, send_sem, recv_sem,
 ):
     length = 2 * NCHAN
     feed = lax.axis_index("feed")
@@ -101,13 +102,21 @@
     def at(ring, plane):
         return lax.rem(ring // 2, 4) * 32 + plane * 2 + lax.rem(ring, 2), ring // 8
 
-    load = pltpu.make_async_copy(basis_ref, basis, load_sem)
-    load.start()
+    loads = [
+        pltpu.make_async_copy(src, dst, load_sem.at[n])
+        for n, (src, dst) in enumerate(
+            ((delay_hbm, delay_ref), (cyl_hbm, cyl_ref), (point_hbm, point_ref), (x_hbm, x_ref), (taps_hbm, taps_ref), (basis_hbm, basis))
+        )
+    ]
+    for load in loads:
+        load.start()
     barrier = pltpu.get_barrier_semaphore()
     for k in range(1, 16):
         for where in (at(ring ^ k, plane), at(ring, plane ^ k)):
             pl.semaphore_signal(barrier, inc=1, device_id=where, device_id_type=MESH)
 
+    for load in loads[:3]:
+        load.wait()
     delay = delay_ref[...].astype(F32)
     cyl = cyl_ref[...].astype(F32)
     for par in range(2):
@@ -119,20 +128,11 @@
         cols[2, pl.ds(g, 16, stride=8), :] = pltpu.roll(cyl, (128 - 16 * g) % 128, 1)
     for q in range(4):
         table[q, 0:4, :] = point_ref[:, q * 128 : q * 128 + 128].astype(F32) * (1.0 / PHASES)
-    fold[...] = jnp.zeros_like(fold)
-
+
+    loads[3].wait()
     pl.semaphore_wait(barrier, 30)
     for k in range(1, 16):
         pl.semaphore_signal(ready, inc=1, device_id=at(ring, plane ^ k), device_id_type=MESH)
-    halo = pltpu.make_async_remote_copy(
-        src_ref=x_ref.at[:, pl.ds(3 * length, 3 * length)], dst_ref=tail,
-        send_sem=halo_send, recv_sem=halo_recv, device_id=(feed, 1), device_id_type=MESH,
-    )
-
-    @pl.when(tm == 0)
-    def _():
-        halo.start()
-        tail[...] = jnp.zeros_like(tail)
 
     def make(step):
         i, half = step // 2, lax.rem(step, 2)
@@ -152,82 +152,113 @@
                     weights[par, q, at_rows, 0:128] = c.astype(BF)
                     weights[par, q, at_rows, 128:256] = s.astype(BF)
 
-    def early(step, carry):
-        make(step)
-        return carry
-
-    lax.fori_loop(0, EARLY, early, 0)
-    load.wait()
-
-    @pl.when(tm == 1)
-    def _():
-        halo.wait_recv()
-
-    for f in range(6):
+    for load in loads[4:]:
+        load.wait()
+    for f in range(9):
         acc = None
         for k in range(TAPS):
             src = f + k - 3
-            if src < 0:
-                piece = tail[:, (src + 3) * length : (src + 4) * length]
-            else:
-                piece = x_ref[:, src * length : (src + 1) * length]
-            term = taps_ref[k : k + 1, :] * piece.astype(F32)
-            acc = term if acc is None else acc + term
+            if 0 <= src < 6:
+                term = taps_ref[k : k + 1, :] * x_ref[:, src * length : (src + 1) * length].astype(F32)
+                acc = term if acc is None else acc + term
         a, b = acc[:, :NCHAN], acc[:, NCHAN:]
         fold[0, f * 16 : f * 16 + 16, :] = a + b
         fold[1, f * 16 : f * 16 + 16, :] = a - b
+    extra = None
     for par in range(2):
         hi, lo = split(fold[par])
         top = basis[0, par]
         out = nt(top, hi) + nt(top, lo) + nt(basis[1, par], hi)
-        sent[par] = out.astype(BF).reshape(NDEV, 2, 128)
-
-    @pl.when(tm == 0)
-    def _():
-        halo.wait_send()
+        sent[:, par, :, :] = out[:, :128].astype(BF).reshape(NDEV, 2, 128)
+        wide[0 : 2 * NDEV, 0:16] = out[:, 128:144]
+        for ri in range(2):
+            spot = 16 * (2 * par + ri)
+            moved = wide[pl.ds(ri, NDEV, stride=2), :]
+            if spot:
+                moved = pltpu.roll(moved, spot, 1)
+            where = lax.broadcasted_iota(jnp.int32, (NDEV, 128), 1) // 16 == 2 * par + ri
+            extra = jnp.where(where, moved, 0.0 if extra is None else extra)
+    wide[pl.ds(0, NDEV, stride=2), :] = extra
+    sent[:, 2, :, :] = wide[0 : 2 * NDEV, :].astype(BF).reshape(NDEV, 2, 128)
+
+    def rest(step, carry):
+        make(step)
+        return carry
 
     pl.semaphore_wait(ready, 15)
 
-    def late(step, carry):
-        for n in range(PER):
-            k = 1 + step * PER + n
-            f, t = lax.rem(feed + k, GROUPS), lax.rem(tm + (feed + k) // GROUPS, 2)
-            pltpu.make_async_remote_copy(
-                src_ref=sent.at[:, t * GROUPS + f], dst_ref=got.at[:, me],
-                send_sem=send_sem.at[0], recv_sem=recv_sem.at[0], device_id=(f, t), device_id_type=MESH,
-            ).start()
-        make(EARLY + step)
-        return carry
-
-    lax.fori_loop(0, 32 - EARLY, late, 0)
-    got[:, me] = sent[:, me]
-    pltpu.make_async_remote_copy(
-        src_ref=sent.at[:, pl.ds(0, NDEV - 1)], dst_ref=got.at[:, pl.ds(0, NDEV - 1)],
-        send_sem=send_sem.at[0], recv_sem=recv_sem.at[0], device_id=(feed, tm), device_id_type=MESH,
-    ).wait()
-
-    for par in range(2):
-        wide[...] = got[par].astype(F32).reshape(2 * NDEV, 128)
+    def start(half, k):
+        to = (me + k * MULT) & (NDEV - 1)
+        f, t = to & (GROUPS - 1), to >> 7
+
+        pltpu.make_async_remote_copy(
+            src_ref=sent.at[to, pl.ds(0, 3 - half)], dst_ref=got.at[me, pl.ds(0, 3 - half)],
+            send_sem=send_sem.at[0], recv_sem=recv_sem.at[half], device_id=(f, t), device_id_type=MESH,
+        ).start()
+
+    for half in range(2):
+
+        @pl.when(tm == half)
+        def _():
+            def group(step, carry):
+                for n in range(PER):
+                    start(half, 1 + step * PER + n)
+                return carry
+
+            lax.fori_loop(0, 255 // PER, group, 0)
+
+    own = [
+        pltpu.make_async_copy(sent.at[me], got.at[me], recv_sem.at[0]),
+        pltpu.make_async_copy(sent.at[me, pl.ds(0, 2)], got.at[me, pl.ds(0, 2)], recv_sem.at[1]),
+    ]
+    for t in range(2):
+        pl.when(tm == t)(own[t].start)
+    lax.fori_loop(0, 32, rest, 0)
+
+    def whole(count, t):
+        size = 3 - t
+        return pltpu.make_async_remote_copy(
+            src_ref=sent.at[pl.ds(0, count), pl.ds(0, size)], dst_ref=got.at[pl.ds(0, count), pl.ds(0, size)],
+            send_sem=send_sem.at[0], recv_sem=recv_sem.at[t], device_id=(feed, tm), device_id_type=MESH,
+        )
+
+    for t in range(2):
+        whole(GROUPS, t).wait_recv()
+        pl.when(tm == t)(whole(NDEV - 1, t).wait_send)
+    for par in range(2):
+        wide[...] = got[:, par].astype(F32).reshape(2 * NDEV, 128)
         for ri in range(2):
             for t in range(2):
                 block = wide[pl.ds(t * 256 + ri, 128, stride=2), :]
-                turned[(ri * 2 + t) * 128 : (ri * 2 + t) * 128 + 128, :] = block.T
+                turned[par, (ri * 2 + t) * 128 : (ri * 2 + t) * 128 + 128, :] = block.T
+    wide[0:256, :] = got[0:GROUPS, 2].astype(F32).reshape(256, 128)
+    block = wide[pl.ds(0, 128, stride=2), :].T
+    for par in range(2):
+        for ri in range(2):
+            turned[par, (ri * 2 + 1) * 128 + 96 : (ri * 2 + 1) * 128 + 112, :] = block[(par * 2 + ri) * 16 : (par * 2 + ri) * 16 + 16]
         for i in range(16):
-            lhs[par, :, i * 128 : i * 128 + 128] = turned[pl.ds(i, 32, stride=16), :].astype(BF)
+            lhs[par, :, i * 128 : i * 128 + 128] = turned[par, pl.ds(i, 32, stride=16), :].astype(BF)
 
     pairs[...] = jnp.zeros_like(pairs)
     scale = 1.0 / math.sqrt(FEEDS)
     lane = lax.broadcasted_iota(jnp.int32, (32, 128), 1) // 32
 
+    unit = lax.broadcasted_iota(jnp.int32, (8, 128), 0)
+
+    def whole_frames(x):
+        first, second = x[:8], x[8:]
+        terms = jnp.where(unit == 2, pltpu.roll(second, 4, 0), pltpu.roll(first, 2, 0))
+        return first * scale, (second + jnp.where(unit < 3, terms, 0.0)) * scale
+
     def chunk(step, carry):
-        q = lax.rem(step + feed // 32, 4)
+        q = (feed // 32 + jnp.where(step == 2, 3, jnp.where(step == 3, 2, step))) & 3
         parts = []
         for par in range(2):
             prod = jnp.dot(lhs[par], weights[par, q], preferred_element_type=F32)
-            real = (prod[:16, :128] - prod[16:, 128:]) * scale
-            imag = (prod[:16, 128:] + prod[16:, :128]) * scale
-            parts.append((real, imag))
-        rows = [parts[par][ri][t * 8 : t * 8 + 8] for t in range(2) for par in range(2) for ri in range(2)]
+            real = prod[:16, :128] - prod[16:, 128:]
+            imag = prod[:16, 128:] + prod[16:, :128]
+            parts.append((whole_frames(real), whole_frames(imag)))
+        rows = [parts[par][ri][t] for t in range(2) for par in range(2) for ri in range(2)]
         flip[...] = jnp.concatenate(rows + [jnp.zeros((64, 128), F32)], axis=0).T
         for t in range(2):
             acc = None
@@ -240,15 +271,15 @@
             packed[pl.ds(t * GROUPS + q * 32, 32)] = pairs[...].astype(BF).reshape(32, 2, 128)
 
         def send(n, carry):
-            v = lax.rem(n + feed, 64)
-            t, f = v // 32, q * 32 + lax.rem(v, 32)
+            v = (n + feed) & 63
+            t, f = v >> 5, q * 32 + (v & 31)
             to = t * GROUPS + f
 
             @pl.when(to != me)
             def _():
                 pltpu.make_async_remote_copy(
                     src_ref=packed.at[to], dst_ref=back_ref.at[me],
-                    send_sem=send_sem.at[1], recv_sem=recv_sem.at[1], device_id=(f, t), device_id_type=MESH,
+                    send_sem=send_sem.at[1], recv_sem=recv_sem.at[2], device_id=(f, t), device_id_type=MESH,
                 ).start()
 
             return carry
@@ -260,7 +291,7 @@
     back_ref[me] = packed[me]
     pltpu.make_async_remote_copy(
         src_ref=packed.at[pl.ds(0, NDEV - 1)], dst_ref=back_ref.at[pl.ds(0, NDEV - 1)],
-        send_sem=send_sem.at[1], recv_sem=recv_sem.at[1], device_id=(feed, tm), device_id_type=MESH,
+        send_sem=send_sem.at[1], recv_sem=recv_sem.at[2], device_id=(feed, tm), device_id_type=MESH,
     ).wait()
 
 
@@ -302,30 +333,32 @@
     back = pl.pallas_call(
         main_kernel,
         out_shape=jax.ShapeDtypeStruct((NDEV, 2, 128), BF),
-        in_specs=[VMEM] * 5 + [pl.BlockSpec(memory_space=pl.ANY)], out_specs=VMEM,
+        in_specs=[pl.BlockSpec(memory_space=pl.ANY)] * 6, out_specs=VMEM,
         scratch_shapes=[
-            pltpu.VMEM((16, 3 * 2 * NCHAN), BF),
+            pltpu.VMEM((16, 6 * 2 * NCHAN), BF),
+            pltpu.VMEM((TAPS, 2 * NCHAN), F32),
+            pltpu.VMEM((16, 128), jnp.int32),
+            pltpu.VMEM((16, 128), jnp.int32),
+            pltpu.VMEM((CYL, BEAMS), jnp.int32),
             pltpu.VMEM((2, 2, NCHAN, NCHAN), BF),
-            pltpu.VMEM((2, 128, NCHAN), F32),
-            pltpu.VMEM((2, NDEV, 2, 128), BF),
-            pltpu.VMEM((2, NDEV, 2, 128), BF),
+            pltpu.VMEM((2, 144, NCHAN), F32),
+            pltpu.VMEM((NDEV, 3, 2, 128), BF),
+            pltpu.VMEM((NDEV, 3, 2, 128), BF),
             pltpu.VMEM((2, 4, FEEDS, 256), BF),
             pltpu.VMEM((3, GROUPS, 128), F32),
             pltpu.VMEM((4, 8, 128), F32),
             pltpu.VMEM((2 * NDEV, 128), F32),
-            pltpu.VMEM((512, 128), F32),
+            pltpu.VMEM((2, 512, 128), F32),
             pltpu.VMEM((2, 32, FEEDS), BF),
             pltpu.VMEM((128, 128), F32),
             pltpu.VMEM((64, 128), F32),
             pltpu.VMEM((NDEV, 2, 128), BF),
-            pltpu.SemaphoreType.DMA,
-            pltpu.SemaphoreType.DMA,
-            pltpu.SemaphoreType.DMA,
+            pltpu.SemaphoreType.DMA((6,)),
             pltpu.SemaphoreType.REGULAR,
             pltpu.SemaphoreType.DMA((2,)),
-            pltpu.SemaphoreType.DMA((2,)),
+            pltpu.SemaphoreType.DMA((3,)),
         ],
-        compiler_params=pltpu.CompilerParams(collective_id=0, has_side_effects=True, vmem_limit_bytes=40 * 2**20),
+        compiler_params=pltpu.CompilerParams(collective_id=0, has_side_effects=True, vmem_limit_bytes=MAIN_VMEM),
     )(samples, filter_taps, feed_delay.reshape(16, 128), feed_cylinder.reshape(16, 128), pointing.T, jnp.asarray(forward_rows()))
     series = pl.pallas_call(
         synth_kernel,

time: 53.3 us -> 43.3 us (0.81)
  Pallas kernels: 47.6 us -> 42.3 us
  local copies, waits for them, and re-layouts: 5.34 us -> 0.9 us
    pallas_call x1, Pallas kernels: 45.8 us -> 40.6 us  [body(): pl.pallas_call(main_kernel, out_shape=jax.ShapeDtypeStruct((NDEV, 2, 128)...]
    unnamed x16 -> x6, local copies, waits for them, and re-layouts: 5.34 us -> 0.9 us
where the time goes in v2:
time: 43.3 us; the launch traced here: 43.2 us
  Pallas kernels  42.3 us (98%)
  local copies, waits for them, and re-layouts  0.9 us (2%)
    pallas_call x1, Pallas kernels, body(): pl.pallas_call(main_kernel, out_shape=jax.ShapeDtypeStruct((NDEV, 2, 128)...  40.6 us
    pallas_call x1, Pallas kernels, body(): pl.pallas_call(synth_kernel, out_shape=jax.ShapeDtypeStruct((6, 4, 2 * NC...  1.72 us
    unnamed x6, local copies, waits for them, and re-layouts  0.9 us

profile of v2, /device:TPU:1, one launch (start us, length us, event | category | flops | bytes accessed | tf_op | source)
XLA Modules:
  0.0 43.2 jit_solution(14311482091939722092)
XLA Ops:
  0.0 0.0 copy-start
  0.0 0.0 copy-start.2
  0.0 40.6 %shard_map.82.q_ref = bf16[256,2,128]{2,1,0:T(2,128)(2,1)} custom-call(bf16[16,6144]{1,0:T(8,128)(2,1)} %x_hbm.1, f32[4,1024]{1,0:T(4,128)} %taps_hbm.1, s32[16,128]{1,0:T(8,128)} %bitcast.4, s32[16,128]{1,0:T(8,128)} %bitcast.5, s32[4,512]{1,0:T(4,128)} %bitcast.6, bf16[2,2,512,512]{3,2,1,0:T(8,128)(2,1)} %constant.4.clone.basis_hbm), custom_call_target="tpu_custom_call" | custom-call | tf_op jit(solution)/shard_map/pallas_call | solution.py:333
  40.6 0.0 copy-done
  40.6 0.0 copy-done.2
  40.6 0.0 copy-start.1
  40.6 0.9 %copy-done.1 = bf16[256,2,128]{2,1,0:T(2,128)(2,1)S(1)} copy-done((bf16[256,2,128]{2,1,0:T(2,128)(2,1)S(1)}, bf16[256,2,128]{2,1,0:T(2,128)(2,1)}, u32[]{:S(2)}) %copy-start.1) | copy-done | bytes 131096
  41.5 1.7 %shard_map.83 = f32[6,4,1024]{2,1,0:T(4,128)} custom-call(bf16[256,2,128]{2,1,0:T(2,128)(2,1)S(1)} %copy-done.1, f32[4]{0:T(128)S(1)} %copy-done.2, bf16[2,2,256,512]{3,2,1,0:T(8,128)(2,1)S(1)} %copy-done), custom_call_target="tpu_custom_call" | custom-call | tf_op jit(solution)/shard_map/pallas_call | solution.py:363
Async XLA Ops:
  0.0 40.6 %copy-start = (bf16[2,2,256,512]{3,2,1,0:T(8,128)(2,1)S(1)}, bf16[2,2,256,512]{3,2,1,0:T(8,128)(2,1)}, u32[]{:S(2)}) copy-start(bf16[2,2,256,512]{3,2,1,0:T(8,128)(2,1)} %constant.5.clone.basis_ref) | copy-start | bytes 3145732
  0.0 40.6 %copy-start.2 = (f32[4]{0:T(128)S(1)}, f32[4]{0:T(128)}, u32[]{:S(2)}) copy-start(f32[4]{0:T(128)} %rate_ref.1) | copy-start | bytes 52
  40.6 0.9 %copy-start.1 = (bf16[256,2,128]{2,1,0:T(2,128)(2,1)S(1)}, bf16[256,2,128]{2,1,0:T(2,128)(2,1)}, u32[]{:S(2)}) copy-start(bf16[256,2,128]{2,1,0:T(2,128)(2,1)} %shard_map.82.q_ref) | copy-start | bytes 393220

commit v3 on v2

--- a/solution.py
+++ b/solution.py
@@ -35,8 +35,7 @@
 SIN_C, COS_C = _fit()
 ROUND = 1.5 * 2.0**23
 MAIN_VMEM = 62 * 2**20
-PER = 17
-MULT = 37
+EARLY = 6
 
 
 def cos_sin(turns):
@@ -88,8 +87,8 @@
 
 
 def main_kernel(
-    x_hbm, taps_hbm, delay_hbm, cyl_hbm, point_hbm, basis_hbm, back_ref,
-    x_ref, taps_ref, delay_ref, cyl_ref, point_ref, basis, fold, sent, got, weights, cols, table, wide, turned, lhs, flip, pairs, packed,
+    x_hbm, taps_hbm, delay_hbm, cyl_hbm, point_hbm, basis_hbm, inverse_hbm, rate_ref, o_ref,
+    x_ref, taps_ref, delay_ref, cyl_ref, point_ref, basis, fold, sent, got, weights, cols, table, wide, turned, lhs, flip, pairs, packed, back_ref, inverse, chirp,
     load_sem, ready, send_sem, recv_sem,
 ):
     length = 2 * NCHAN
@@ -100,12 +99,12 @@
     ring = tm * 8 + feed // 32 * 2 + lax.rem(feed, 2)
 
     def at(ring, plane):
-        return lax.rem(ring // 2, 4) * 32 + plane * 2 + lax.rem(ring, 2), ring // 8
+        return ((ring >> 1) & 3) * 32 + plane * 2 + (ring & 1), ring >> 3
 
     loads = [
         pltpu.make_async_copy(src, dst, load_sem.at[n])
         for n, (src, dst) in enumerate(
-            ((delay_hbm, delay_ref), (cyl_hbm, cyl_ref), (point_hbm, point_ref), (x_hbm, x_ref), (taps_hbm, taps_ref), (basis_hbm, basis))
+            ((delay_hbm, delay_ref), (cyl_hbm, cyl_ref), (point_hbm, point_ref), (x_hbm, x_ref), (taps_hbm, taps_ref), (basis_hbm, basis), (inverse_hbm, inverse))
         )
     ]
     for load in loads:
@@ -128,11 +127,6 @@
         cols[2, pl.ds(g, 16, stride=8), :] = pltpu.roll(cyl, (128 - 16 * g) % 128, 1)
     for q in range(4):
         table[q, 0:4, :] = point_ref[:, q * 128 : q * 128 + 128].astype(F32) * (1.0 / PHASES)
-
-    loads[3].wait()
-    pl.semaphore_wait(barrier, 30)
-    for k in range(1, 16):
-        pl.semaphore_signal(ready, inc=1, device_id=at(ring, plane ^ k), device_id_type=MESH)
 
     def make(step):
         i, half = step // 2, lax.rem(step, 2)
@@ -149,10 +143,10 @@
                 for par, t in ((0, t0), (1, t1)):
                     c, s = cos_sin(t * steer)
                     at_rows = pl.ds(pl.multiple_of(i * 128 + rc * 32, 32), 32)
-                    weights[par, q, at_rows, 0:128] = c.astype(BF)
-                    weights[par, q, at_rows, 128:256] = s.astype(BF)
-
-    for load in loads[4:]:
+                    weights[par, q, 0, at_rows, :] = c.astype(BF)
+                    weights[par, q, 1, at_rows, :] = s.astype(BF)
+
+    for load in loads[3:6]:
         load.wait()
     for f in range(9):
         acc = None
@@ -181,31 +175,44 @@
     wide[pl.ds(0, NDEV, stride=2), :] = extra
     sent[:, 2, :, :] = wide[0 : 2 * NDEV, :].astype(BF).reshape(NDEV, 2, 128)
 
+    pl.semaphore_wait(barrier, 30)
+    for k in range(1, 16):
+        pl.semaphore_signal(ready, inc=1, device_id=at(ring, plane ^ k), device_id_type=MESH)
+
     def rest(step, carry):
         make(step)
         return carry
 
-    pl.semaphore_wait(ready, 15)
-
-    def start(half, k):
-        to = (me + k * MULT) & (NDEV - 1)
-        f, t = to & (GROUPS - 1), to >> 7
-
+    def start(half, where):
+        f, t = where
         pltpu.make_async_remote_copy(
-            src_ref=sent.at[to, pl.ds(0, 3 - half)], dst_ref=got.at[me, pl.ds(0, 3 - half)],
-            send_sem=send_sem.at[0], recv_sem=recv_sem.at[half], device_id=(f, t), device_id_type=MESH,
+            src_ref=sent.at[t * GROUPS + f, pl.ds(0, 3 - half)], dst_ref=got.at[me, pl.ds(0, 3 - half)],
+            send_sem=send_sem.at[0], recv_sem=recv_sem.at[half], device_id=where, device_id_type=MESH,
         ).start()
 
     for half in range(2):
 
         @pl.when(tm == half)
         def _():
-            def group(step, carry):
-                for n in range(PER):
-                    start(half, 1 + step * PER + n)
+            def known(k, carry):
+                start(half, at(ring ^ k, plane))
+                start(half, at(ring, plane ^ k))
                 return carry
 
-            lax.fori_loop(0, 255 // PER, group, 0)
+            lax.fori_loop(1, 16, known, 0, unroll=5)
+
+    lax.fori_loop(0, EARLY, rest, 0)
+    pl.semaphore_wait(ready, 15)
+    for half in range(2):
+
+        @pl.when(tm == half)
+        def _():
+            def far(k, carry):
+                for n in range(1, 16):
+                    start(half, at(ring ^ k, plane ^ n))
+                return carry
+
+            lax.fori_loop(1, 16, far, 0)
 
     own = [
         pltpu.make_async_copy(sent.at[me], got.at[me], recv_sem.at[0]),
@@ -213,7 +220,8 @@
     ]
     for t in range(2):
         pl.when(tm == t)(own[t].start)
-    lax.fori_loop(0, 32, rest, 0)
+
+    lax.fori_loop(EARLY, 32, rest, 0)
 
     def whole(count, t):
         size = 3 - t
@@ -250,11 +258,14 @@
         terms = jnp.where(unit == 2, pltpu.roll(second, 4, 0), pltpu.roll(first, 2, 0))
         return first * scale, (second + jnp.where(unit < 3, terms, 0.0)) * scale
 
-    def chunk(step, carry):
-        q = (feed // 32 + jnp.where(step == 2, 3, jnp.where(step == 3, 2, step))) & 3
+    def part(step):
+        return (feed // 32 + jnp.where(step == 2, 3, jnp.where(step == 3, 2, step))) & 3
+
+    def chunk(q):
         parts = []
         for par in range(2):
-            prod = jnp.dot(lhs[par], weights[par, q], preferred_element_type=F32)
+            both = jnp.concatenate([weights[par, q, 0], weights[par, q, 1]], axis=1)
+            prod = jnp.dot(lhs[par], both, preferred_element_type=F32)
             real = prod[:16, :128] - prod[16:, 128:]
             imag = prod[:16, 128:] + prod[16:, :128]
             parts.append((whole_frames(real), whole_frames(imag)))
@@ -270,70 +281,80 @@
             pairs[pl.ds(0, 32, stride=2), :] = acc
             packed[pl.ds(t * GROUPS + q * 32, 32)] = pairs[...].astype(BF).reshape(32, 2, 128)
 
-        def send(n, carry):
-            v = (n + feed) & 63
-            t, f = v >> 5, q * 32 + (v & 31)
-            to = t * GROUPS + f
-
-            @pl.when(to != me)
-            def _():
-                pltpu.make_async_remote_copy(
-                    src_ref=packed.at[to], dst_ref=back_ref.at[me],
-                    send_sem=send_sem.at[1], recv_sem=recv_sem.at[2], device_id=(f, t), device_id_type=MESH,
-                ).start()
-
-            return carry
-
-        lax.fori_loop(0, 64, send, 0, unroll=16)
+    def send(q, n):
+        v = (n + feed) & 63
+        t, f = v >> 5, q * 32 + (v & 31)
+        to = t * GROUPS + f
+
+        @pl.when(to != me)
+        def _():
+            pltpu.make_async_remote_copy(
+                src_ref=packed.at[to], dst_ref=back_ref.at[me],
+                send_sem=send_sem.at[1], recv_sem=recv_sem.at[2], device_id=(f, t), device_id_type=MESH,
+            ).start()
+
+    def later(step, carry):
+        for n in range(64):
+            send(part(step - 1), n)
+        chunk(part(step))
         return carry
 
-    lax.fori_loop(0, 4, chunk, 0)
+    def last(n, carry):
+        send(part(jnp.int32(3)), n)
+        return carry
+
+    chunk(part(jnp.int32(0)))
+    lax.fori_loop(1, 4, later, 0)
+    lax.fori_loop(0, 64, last, 0, unroll=16)
     back_ref[me] = packed[me]
+    pos_ids = lax.broadcasted_iota(jnp.int32, (8, 256), 1)
+    for par in range(2):
+        pos = (2 * pos_ids + par).astype(F32) * (1.0 / NCHAN)
+        for b in range(4):
+            chirp[par, b, 0], chirp[par, b, 1] = cos_sin((0.5 * rate_ref[b]) * (pos * pos))
+    loads[6].wait()
     pltpu.make_async_remote_copy(
         src_ref=packed.at[pl.ds(0, NDEV - 1)], dst_ref=back_ref.at[pl.ds(0, NDEV - 1)],
         send_sem=send_sem.at[1], recv_sem=recv_sem.at[2], device_id=(feed, tm), device_id_type=MESH,
     ).wait()
 
-
-def synth_kernel(q_ref, rate_ref, basis_ref, o_ref, wide, turned):
-    wide[...] = q_ref[...].astype(F32).reshape(2 * NDEV, 128)
+    wide[...] = back_ref[...].astype(F32).reshape(2 * NDEV, 128)
     for h in range(2):
-        turned[:, h * 128 : h * 128 + 128] = wide[pl.ds(h * 256, 128, stride=2), :].T
-    s = lax.broadcasted_iota(jnp.int32, (8, 256), 1)
+        turned[1, h * 128 : h * 128 + 128, :] = wide[pl.ds(h * 256, 128, stride=2), :].T
     halves = []
     for par in range(2):
-        pos = (2 * s + par).astype(F32) * (1.0 / NCHAN)
         real, imag = [], []
         for b in range(4):
-            c, sn = cos_sin((0.5 * rate_ref[b]) * (pos * pos))
-            at = b * 32 + par * 16
-            xr = turned[at : at + 8, :]
-            xi = turned[at + 8 : at + 16, :]
+            spot = b * 32 + par * 16
+            xr, xi = [
+                jnp.concatenate([turned[1, h * 128 + spot + o : h * 128 + spot + o + 8, :] for h in range(2)], axis=1)
+                for o in (0, 8)
+            ]
+            c, sn = chirp[par, b, 0], chirp[par, b, 1]
             real.append(xr * c - xi * sn)
             imag.append(xr * sn + xi * c)
-        both = jnp.concatenate(real + imag, axis=0)
-        hi, lo = split(both)
-        top = basis_ref[0, par]
+        hi, lo = split(jnp.concatenate(real + imag, axis=0))
+        top = inverse[0, par]
         prod = (
             jnp.dot(hi, top, preferred_element_type=F32)
             + jnp.dot(lo, top, preferred_element_type=F32)
-            + jnp.dot(hi, basis_ref[1, par], preferred_element_type=F32)
+            + jnp.dot(hi, inverse[1, par], preferred_element_type=F32)
         )
         halves.append((prod[:32, :256] - prod[32:, 256:], prod[:32, 256:] + prod[32:, :256]))
-    (er, ei), (orr, oi) = halves
+    (er, ei), (sr, si) = halves
     for b in range(4):
         rows = slice(b * 8, b * 8 + 6)
-        o_ref[:, b, 0:256] = er[rows] + orr[rows]
-        o_ref[:, b, 256:512] = er[rows] - orr[rows]
-        o_ref[:, b, 512:768] = ei[rows] + oi[rows]
-        o_ref[:, b, 768:1024] = ei[rows] - oi[rows]
+        o_ref[:, b, 0:256] = er[rows] + sr[rows]
+        o_ref[:, b, 256:512] = er[rows] - sr[rows]
+        o_ref[:, b, 512:768] = ei[rows] + si[rows]
+        o_ref[:, b, 768:1024] = ei[rows] - si[rows]
 
 
 def body(samples, filter_taps, feed_cylinder, feed_delay, pointing, chirp_rate):
-    back = pl.pallas_call(
+    series = pl.pallas_call(
         main_kernel,
-        out_shape=jax.ShapeDtypeStruct((NDEV, 2, 128), BF),
-        in_specs=[pl.BlockSpec(memory_space=pl.ANY)] * 6, out_specs=VMEM,
+        out_shape=jax.ShapeDtypeStruct((6, 4, 2 * NCHAN), F32),
+        in_specs=[pl.BlockSpec(memory_space=pl.ANY)] * 7 + [pl.BlockSpec(memory_space=pltpu.SMEM)], out_specs=VMEM,
         scratch_shapes=[
             pltpu.VMEM((16, 6 * 2 * NCHAN), BF),
             pltpu.VMEM((TAPS, 2 * NCHAN), F32),
@@ -344,7 +365,7 @@
             pltpu.VMEM((2, 144, NCHAN), F32),
             pltpu.VMEM((NDEV, 3, 2, 128), BF),
             pltpu.VMEM((NDEV, 3, 2, 128), BF),
-            pltpu.VMEM((2, 4, FEEDS, 256), BF),
+            pltpu.VMEM((2, 4, 2, FEEDS, 128), BF),
             pltpu.VMEM((3, GROUPS, 128), F32),
             pltpu.VMEM((4, 8, 128), F32),
             pltpu.VMEM((2 * NDEV, 128), F32),
@@ -353,20 +374,16 @@
             pltpu.VMEM((128, 128), F32),
             pltpu.VMEM((64, 128), F32),
             pltpu.VMEM((NDEV, 2, 128), BF),
-            pltpu.SemaphoreType.DMA((6,)),
+            pltpu.VMEM((NDEV, 2, 128), BF),
+            pltpu.VMEM((2, 2, NCHAN // 2, NCHAN), BF),
+            pltpu.VMEM((2, 4, 2, 8, 256), F32),
+            pltpu.SemaphoreType.DMA((7,)),
             pltpu.SemaphoreType.REGULAR,
             pltpu.SemaphoreType.DMA((2,)),
             pltpu.SemaphoreType.DMA((3,)),
         ],
         compiler_params=pltpu.CompilerParams(collective_id=0, has_side_effects=True, vmem_limit_bytes=MAIN_VMEM),
-    )(samples, filter_taps, feed_delay.reshape(16, 128), feed_cylinder.reshape(16, 128), pointing.T, jnp.asarray(forward_rows()))
-    series = pl.pallas_call(
-        synth_kernel,
-        out_shape=jax.ShapeDtypeStruct((6, 4, 2 * NCHAN), F32),
-        in_specs=[VMEM, pl.BlockSpec(memory_space=pltpu.SMEM), VMEM], out_specs=VMEM,
-        scratch_shapes=[pltpu.VMEM((2 * NDEV, 128), F32), pltpu.VMEM((128, 256), F32)],
-        compiler_params=pltpu.CompilerParams(vmem_limit_bytes=16 * 2**20),
-    )(back, chirp_rate, jnp.asarray(inverse_rows()))
+    )(samples, filter_taps, feed_delay.reshape(16, 128), feed_cylinder.reshape(16, 128), pointing.T, jnp.asarray(forward_rows()), jnp.asarray(inverse_rows()), chirp_rate)
     return jnp.transpose(series, (1, 0, 2))
 
 

time: 43.3 us -> 41.1 us (0.949)
  Pallas kernels: 42.3 us -> 39.5 us
  local copies, waits for them, and re-layouts: 0.9 us -> 1.54 us
    pallas_call x2 -> x1, Pallas kernels: 42.3 us -> 39.5 us  [body(): pl.pallas_call(main_kernel, out_shape=jax.ShapeDtypeStruct((6, 4, 2 * NCH...]
    unnamed x6 -> x1, local copies, waits for them, and re-layouts: 0.9 us -> 1.54 us
where the time goes in v3:
time: 41.1 us; the launch traced here: 41 us
  Pallas kernels  39.5 us (96%)
  local copies, waits for them, and re-layouts  1.54 us (4%)
    pallas_call x1, Pallas kernels, body(): pl.pallas_call(main_kernel, out_shape=jax.ShapeDtypeStruct((6, 4, 2 * NCH...  39.5 us
    unnamed x1, local copies, waits for them, and re-layouts  1.54 us

profile of v3, /device:TPU:1, one launch (start us, length us, event | category | flops | bytes accessed | tf_op | source)
XLA Modules:
  0.0 41.0 jit_solution(9196504274345366184)
XLA Ops:
  0.0 39.5 %shard_map.82 = f32[6,4,1024]{2,1,0:T(4,128)} custom-call(bf16[16,6144]{1,0:T(8,128)(2,1)} %x_hbm.1, f32[4,1024]{1,0:T(4,128)} %taps_hbm.1, s32[16,128]{1,0:T(8,128)} %bitcast.5, s32[16,128]{1,0:T(8,128)} %bitcast.6, s32[4,512]{1,0:T(4,128)} %bitcast.7, bf16[2,2,512,512]{3,2,1,0:T(8,128)(2,1)} %constant.4.clone.basis_hbm, ...), custom_call_target="tpu_custom_call" | custom-call | tf_op jit(solution)/shard_map/pallas_call | solution.py:354
  39.5 1.5 %copy.10 = f32[4,6,1024]{2,0,1:T(4,128)} copy(f32[4,6,1024]{2,0,1:T(4,128)} %bitcast.4) | data formatting | bytes 196608

commit v4 on v3

--- a/solution.py
+++ b/solution.py
@@ -232,12 +232,11 @@
 
     for t in range(2):
         whole(GROUPS, t).wait_recv()
-        pl.when(tm == t)(whole(NDEV - 1, t).wait_send)
-    for par in range(2):
-        wide[...] = got[:, par].astype(F32).reshape(2 * NDEV, 128)
-        for ri in range(2):
-            for t in range(2):
-                block = wide[pl.ds(t * 256 + ri, 128, stride=2), :]
+        for par in range(2):
+            here = slice(t * GROUPS, t * GROUPS + GROUPS)
+            wide[par * 256 : par * 256 + 256, :] = got[here, par].astype(F32).reshape(256, 128)
+            for ri in range(2):
+                block = wide[pl.ds(par * 256 + ri, 128, stride=2), :]
                 turned[par, (ri * 2 + t) * 128 : (ri * 2 + t) * 128 + 128, :] = block.T
     wide[0:256, :] = got[0:GROUPS, 2].astype(F32).reshape(256, 128)
     block = wide[pl.ds(0, 128, stride=2), :].T
@@ -318,6 +317,8 @@
         send_sem=send_sem.at[1], recv_sem=recv_sem.at[2], device_id=(feed, tm), device_id_type=MESH,
     ).wait()
 
+    for t in range(2):
+        pl.when(tm == t)(whole(NDEV - 1, t).wait_send)
     wide[...] = back_ref[...].astype(F32).reshape(2 * NDEV, 128)
     for h in range(2):
         turned[1, h * 128 : h * 128 + 128, :] = wide[pl.ds(h * 256, 128, stride=2), :].T

time: 41.1 us -> 41.2 us (level)
  no operation moved by 1% of the time
where the time goes in v4:
time: 41.2 us; the launch traced here: 41 us
  Pallas kernels  39.5 us (96%)
  local copies, waits for them, and re-layouts  1.54 us (4%)
    pallas_call x1, Pallas kernels, body(): pl.pallas_call(main_kernel, out_shape=jax.ShapeDtypeStruct((6, 4, 2 * NCH...  39.5 us
    unnamed x1, local copies, waits for them, and re-layouts  1.54 us

profile of v4, /device:TPU:1, one launch (start us, length us, event | category | flops | bytes accessed | tf_op | source)
XLA Modules:
  0.0 41.0 jit_solution(2521066962355616578)
XLA Ops:
  0.0 39.5 %shard_map.82 = f32[6,4,1024]{2,1,0:T(4,128)} custom-call(bf16[16,6144]{1,0:T(8,128)(2,1)} %x_hbm.1, f32[4,1024]{1,0:T(4,128)} %taps_hbm.1, s32[16,128]{1,0:T(8,128)} %bitcast.5, s32[16,128]{1,0:T(8,128)} %bitcast.6, s32[4,512]{1,0:T(4,128)} %bitcast.7, bf16[2,2,512,512]{3,2,1,0:T(8,128)(2,1)} %constant.4.clone.basis_hbm, ...), custom_call_target="tpu_custom_call" | custom-call | tf_op jit(solution)/shard_map/pallas_call | solution.py:355
  39.5 1.5 %copy.10 = f32[4,6,1024]{2,0,1:T(4,128)} copy(f32[4,6,1024]{2,0,1:T(4,128)} %bitcast.4) | data formatting | bytes 196608
